TPU v7x, 32 devices: a whole 2x2x4 slice. The times are simulated.
32 devices in a mesh: dap: 8 (over z, core), ch: 4 (over y, x).
Axes of the slice: x: 2, y: 2, z: 4, core: 2. Of those that a mesh axis runs over, the one named last changes fastest.
Arguments:
- pair_rep: bfloat16 [120, 120, 128], P('dap', 'ch'), may hold values from -400 to 400
- residue_mask: int32 [120], replicated, may hold values 0 or 1
- w_proj: bfloat16 [128, 512], replicated, may hold values from -0.5 to 0.5
- w_gate: bfloat16 [128, 128], replicated, may hold values from -0.5 to 0.5
- w_out: bfloat16 [128, 128], replicated, may hold values from -0.5 to 0.5
- cotangent: bfloat16 [120, 120, 128], P('dap', 'ch'), may hold values from -6 to 6
Outputs:
- pair_update: bfloat16 [120, 120, 128], P('dap', 'ch')
- grad_pair: bfloat16 [120, 120, 128], P('dap', 'ch')
Inputs may be any that keep to these rules, and one draw needn't show every extreme that they name: `residue_mask`: 1 marks a residue of the crop, 0 a padding position.
All inputs are finite; a program needn't handle non-finite values.
Results may differ from a plain program's by a relative error of at most 0.0085.
Values may be sent and summed in bfloat16 or wider, within the bound.
No kernel may reach another device: no remote copies, remote signals or barrier semaphores. Data moves between devices by JAX's collectives and lax.ppermute only.
A program may use at most 64 MiB of HBM per device.

v0:
```python
import jax
import jax.numpy as jnp
from jax import lax
from jax.sharding import PartitionSpec as P

EPSILON = 1e-05


def normalize(values, axis):
    center = jnp.mean(values, axis=axis, keepdims=True)
    spread = values - center
    scale_inv = lax.rsqrt(jnp.mean(spread * spread, axis=axis, keepdims=True) + EPSILON)
    return (spread * scale_inv, scale_inv)


def norm_back(grad_in, normed, scale_inv, axis):
    first = jnp.mean(grad_in, axis=axis, keepdims=True)
    second = jnp.mean(grad_in * normed, axis=axis, keepdims=True)
    return scale_inv * (grad_in - first - normed * second)


def on_device(pair_rep, residue_mask, w_proj, w_gate, w_out, cotangent):
    row_count, columns, channels = pair_rep.shape
    hidden_width = w_out.shape[0]
    row_start = lax.axis_index("dap") * row_count
    col_start = lax.axis_index("ch") * columns
    live_flags = residue_mask.astype(jnp.float32)
    row_live = lax.dynamic_slice_in_dim(live_flags, row_start, row_count, 0)
    col_live = lax.dynamic_slice_in_dim(live_flags, col_start, columns, 0)
    cell_mask = row_live[:, None] * col_live[None, :]
    normed, pair_scale = normalize(pair_rep.astype(jnp.float32), 2)
    normed_half = normed.astype(jnp.bfloat16)
    projected = jnp.einsum("rkd,de->erk", normed_half, w_proj, preferred_element_type=jnp.float32)
    left_sig = jax.nn.sigmoid(projected[:hidden_width])
    left_val = projected[hidden_width : 2 * hidden_width]
    right_sig = jax.nn.sigmoid(projected[2 * hidden_width : 3 * hidden_width])
    right_val = projected[3 * hidden_width :]
    left_cells = (left_sig * left_val * cell_mask).astype(jnp.bfloat16)
    right_cells = (right_sig * right_val * cell_mask).astype(jnp.bfloat16)
    gate_values = jax.nn.sigmoid(
        jnp.einsum("rkd,de->rke", normed_half, w_gate, preferred_element_type=jnp.float32)
    )
    left_rows, right_rows = (
        lax.all_to_all(left_cells, "ch", split_axis=0, concat_axis=2, tiled=True),
        lax.all_to_all(right_cells, "ch", split_axis=0, concat_axis=2, tiled=True),
    )
    product = jnp.einsum(
        "cik,cjk->cij",
        left_rows,
        lax.all_gather(right_rows, "dap", axis=1, tiled=True),
        preferred_element_type=jnp.float32,
    ).astype(jnp.bfloat16)
    product_cells = lax.all_to_all(product, "ch", split_axis=2, concat_axis=0, tiled=True)
    hidden_norm, hidden_scale = normalize(product_cells.astype(jnp.float32), 0)
    hidden_half = hidden_norm.astype(jnp.bfloat16)
    projected_out = jnp.einsum(
        "hrk,hd->rkd", hidden_half, w_out, preferred_element_type=jnp.float32
    )
    pair_update = (gate_values * projected_out).astype(jnp.bfloat16)
    upstream = cotangent.astype(jnp.float32)
    grad_out = (upstream * gate_values).astype(jnp.bfloat16)
    grad_logit = (upstream * projected_out * gate_values * (1.0 - gate_values)).astype(jnp.bfloat16)
    grad_hidden = jnp.einsum("rkd,hd->hrk", grad_out, w_out, preferred_element_type=jnp.float32)
    grad_product = norm_back(grad_hidden, hidden_norm, hidden_scale, 0).astype(jnp.bfloat16)
    grad_rows = lax.all_to_all(grad_product, "ch", split_axis=0, concat_axis=2, tiled=True)
    piece_left = lax.all_gather(left_rows, "dap", axis=1, tiled=True)
    piece_right = lax.all_gather(right_rows, "dap", axis=1, tiled=True)
    piece_grad = lax.all_gather(grad_rows, "dap", axis=1, tiled=True)
    cross_slab = lax.dynamic_slice_in_dim(piece_grad, row_start, row_count, 2)
    new_left = jnp.einsum(
        "cij,cjk->cik", grad_rows, piece_right, preferred_element_type=jnp.float32
    )
    new_right = jnp.einsum(
        "cij,cik->cjk", cross_slab, piece_left, preferred_element_type=jnp.float32
    )
    left_back, right_back = (
        lax.all_to_all(
            new_left.astype(jnp.bfloat16), "ch", split_axis=2, concat_axis=0, tiled=True
        ),
        lax.all_to_all(
            new_right.astype(jnp.bfloat16), "ch", split_axis=2, concat_axis=0, tiled=True
        ),
    )
    masked_left = left_back.astype(jnp.float32) * cell_mask
    masked_right = right_back.astype(jnp.float32) * cell_mask
    grad_proj = jnp.concatenate(
        [
            masked_left * left_val * left_sig * (1.0 - left_sig),
            masked_left * left_sig,
            masked_right * right_val * right_sig * (1.0 - right_sig),
            masked_right * right_sig,
        ],
        axis=0,
    ).astype(jnp.bfloat16)
    grad_normed = jnp.einsum("erk,de->rkd", grad_proj, w_proj, preferred_element_type=jnp.float32)
    grad_normed = grad_normed + jnp.einsum(
        "rke,de->rkd", grad_logit, w_gate, preferred_element_type=jnp.float32
    )
    grad_pair = norm_back(grad_normed, normed, pair_scale, 2).astype(jnp.bfloat16)
    return (pair_update, grad_pair)


def solution(mesh):
    return jax.shard_map(
        on_device,
        mesh=mesh,
        in_specs=(P("dap", "ch", None), P(), P(), P(), P(), P("dap", "ch", None)),
        out_specs=(P("dap", "ch", None), P("dap", "ch", None)),
        check_vma=False,
    )
```

profile of v0, /device:TPU:0, one launch (start us, length us, event | category | flops | bytes accessed | tf_op | source)
XLA Modules:
  0.0 124.0 jit_solution(5858120735575920195)
XLA Ops:
  0.7 1.1 convert_reduce_fusion
  3.9 1.3 %reshape.95 = bf16[4,2,7200]{2,1,0:T(2,128)(2,1)} reshape(bf16[128,15,30]{2,1,0:T(8,128)(2,1)S(1)} %copy.73) | data formatting | bytes 230400
  5.2 5.2 %all-to-all-start.1 = ((bf16[4,2,7200]{2,1,0:T(2,128)(2,1)}), bf16[4,2,7200]{2,1,0:T(2,128)(2,1)S(1)}, u32[]{:S(2)}, u32[]{:S(2)}) async-start(bf16[4,2,7200]{2,1,0:T(2,128)(2,1)} %reshape.95), calls=%async_computation.1 | async-start | bytes 233472 | tf_op jit(solution)/shard_map/all_to_all | solution.py:45
  10.9 1.3 %reshape.97 = bf16[4,2,7200]{2,1,0:T(2,128)(2,1)} reshape(bf16[128,15,30]{2,1,0:T(8,128)(2,1)S(1)} %copy.71) | data formatting | bytes 230400
  12.2 3.2 %all-to-all-done.1 = bf16[4,2,7200]{2,1,0:T(2,128)(2,1)S(1)} async-done(((bf16[4,2,7200]{2,1,0:T(2,128)(2,1)}), bf16[4,2,7200]{2,1,0:T(2,128)(2,1)S(1)}, u32[]{:S(2)}, u32[]{:S(2)}) %all-to-all-start.1) | async-done | bytes 115232 | tf_op jit(solution)/shard_map/all_to_all | solution.py:45
  15.4 3.3 %all-to-all-start = ((bf16[4,2,7200]{2,1,0:T(2,128)(2,1)}), bf16[4,2,7200]{2,1,0:T(2,128)(2,1)S(1)}, u32[]{:S(2)}, u32[]{:S(2)}) async-start(bf16[4,2,7200]{2,1,0:T(2,128)(2,1)} %reshape.97), calls=%async_computation | async-start | bytes 233472 | tf_op jit(solution)/shard_map/all_to_all | solution.py:44
  20.0 17.0 %all_gather.10 = bf16[32,120,120]{2,0,1:T(8,128)(2,1)S(1)} all-gather(bf16[32,15,120]{2,0,1:T(8,128)(2,1)S(1)} %all_to_all.67), channel_id=1, replica_groups=mesh['dap'=8,'ch'=4] {'dap'}, dimensions={1}, use_global_device_ids=true | all-gather | bytes 1036800 | tf_op jit(solution)/shard_map/all_gather | solution.py:50
  39.7 8.9 %all_to_all.81 = bf16[4,2,7200]{2,1,0:T(2,128)(2,1)S(1)} all-to-all(bf16[4,2,7200]{2,1,0:T(2,128)(2,1)S(1)} %reshape.99), channel_id=1, replica_groups=mesh['dap'=8,'ch'=4] {'ch'}, dimensions={0} | all-to-all | bytes 230400 | tf_op jit(solution)/shard_map/all_to_all | solution.py:53
  49.2 1.0 copy.78
  50.2 1.3 %reshape.89 = f32[32,15,4,30]{3,2,0,1:T(4,128)S(1)} reshape(bf16[32,15,120]{2,0,1:T(8,128)(2,1)} %copy.78) | data formatting | bytes 345600 | tf_op jit(solution)/shard_map/convert_element_type | solution.py:54
  51.7 1.7 %copy.79 = f32[4,32,15,30]{1,0,3,2:T(4,128)} copy(f32[4,32,15,30]{3,0,1,2:T(4,128)S(1)} %bitcast.66) | data formatting | bytes 460800 | tf_op jit(solution)/shard_map/convert_element_type | solution.py:54
  53.5 1.6 %reshape.85 = f32[128,15,30]{0,2,1:T(8,128)S(1)} reshape(f32[4,32,15,30]{1,0,3,2:T(4,128)} %copy.79) | data formatting | bytes 460800 | tf_op jit(solution)/shard_map/convert_element_type | solution.py:54
  59.1 1.3 %reshape.101 = bf16[4,2,7200]{2,1,0:T(2,128)(2,1)} reshape(bf16[128,15,30]{2,1,0:T(8,128)(2,1)S(1)} %copy.80) | data formatting | bytes 230400
  60.4 3.4 %all-to-all-start.3 = ((bf16[4,2,7200]{2,1,0:T(2,128)(2,1)}), bf16[4,2,7200]{2,1,0:T(2,128)(2,1)S(1)}, u32[]{:S(2)}, u32[]{:S(2)}) async-start(bf16[4,2,7200]{2,1,0:T(2,128)(2,1)} %reshape.101), calls=%async_computation.3 | async-start | bytes 233472 | tf_op jit(solution)/shard_map/all_to_all | solution.py:65
  63.8 16.8 %all_gather.12 = bf16[32,120,120]{2,0,1:T(8,128)(2,1)} all-gather(bf16[32,15,120]{2,0,1:T(8,128)(2,1)S(1)} %copy-done.3), channel_id=1, replica_groups=mesh['dap'=8,'ch'=4] {'dap'}, dimensions={1}, use_global_device_ids=true | all-gather | bytes 1036800 | tf_op jit(solution)/shard_map/all_gather | solution.py:66
  82.4 16.5 %all_gather.11 = bf16[32,120,120]{2,0,1:T(8,128)(2,1)S(1)} all-gather(bf16[32,15,120]{2,0,1:T(8,128)(2,1)S(1)} %all_to_all.72), channel_id=1, replica_groups=mesh['dap'=8,'ch'=4] {'dap'}, dimensions={1}, use_global_device_ids=true | all-gather | bytes 1036800 | tf_op jit(solution)/shard_map/all_gather | solution.py:68
  99.4 1.1 reshape.105
  100.5 4.2 %all-to-all-start.4 = ((bf16[4,2,7200]{2,1,0:T(2,128)(2,1)}), bf16[4,2,7200]{2,1,0:T(2,128)(2,1)S(1)}, u32[]{:S(2)}, u32[]{:S(2)}) async-start(bf16[4,2,7200]{2,1,0:T(2,128)(2,1)} %reshape.105), calls=%async_computation.4 | async-start | bytes 233472 | tf_op jit(solution)/shard_map/all_to_all | solution.py:77
  107.0 1.1 reshape.103
  108.1 1.5 %all-to-all-done.4 = bf16[4,2,7200]{2,1,0:T(2,128)(2,1)S(1)} async-done(((bf16[4,2,7200]{2,1,0:T(2,128)(2,1)}), bf16[4,2,7200]{2,1,0:T(2,128)(2,1)S(1)}, u32[]{:S(2)}, u32[]{:S(2)}) %all-to-all-start.4) | async-done | bytes 115232 | tf_op jit(solution)/shard_map/all_to_all | solution.py:77
  109.7 3.5 %all-to-all-start.5 = ((bf16[4,2,7200]{2,1,0:T(2,128)(2,1)}), bf16[4,2,7200]{2,1,0:T(2,128)(2,1)S(1)}, u32[]{:S(2)}, u32[]{:S(2)}) async-start(bf16[4,2,7200]{2,1,0:T(2,128)(2,1)} %reshape.103), calls=%async_computation.5 | async-start | bytes 233472 | tf_op jit(solution)/shard_map/all_to_all | solution.py:80
  114.5 1.5 %copy.86 = f32[4,32,15,30]{1,0,3,2:T(4,128)S(1)} copy(f32[4,32,15,30]{3,0,1,2:T(4,128)S(1)} %bitcast.67) | data formatting | bytes 460800 | tf_op jit(solution)/shard_map/convert_element_type | solution.py:84
  116.5 1.5 %all-to-all-done.5 = bf16[4,2,7200]{2,1,0:T(2,128)(2,1)S(1)} async-done(((bf16[4,2,7200]{2,1,0:T(2,128)(2,1)}), bf16[4,2,7200]{2,1,0:T(2,128)(2,1)S(1)}, u32[]{:S(2)}, u32[]{:S(2)}) %all-to-all-start.5) | async-done | bytes 115232 | tf_op jit(solution)/shard_map/all_to_all | solution.py:80
  119.3 1.5 %copy.91 = f32[4,32,15,30]{1,0,3,2:T(4,128)S(1)} copy(f32[4,32,15,30]{3,0,1,2:T(4,128)S(1)} %bitcast.68) | data formatting | bytes 460800 | tf_op jit(solution)/shard_map/convert_element_type | solution.py:85
  (83 shorter events, 21.9 us)
Async XLA Ops:
  0.6 2.2 %copy-start = (bf16[128,512]{1,0:T(8,128)(2,1)S(1)}, bf16[128,512]{1,0:T(8,128)(2,1)}, u32[]{:S(2)}) copy-start(bf16[128,512]{1,0:T(8,128)(2,1)} %param.8) | copy-start | bytes 393220
  0.6 1.1 copy-start.1
  2.0 0.7 copy-start.13
  5.2 10.2 %all-to-all-start.1 = ((bf16[4,2,7200]{2,1,0:T(2,128)(2,1)}), bf16[4,2,7200]{2,1,0:T(2,128)(2,1)S(1)}, u32[]{:S(2)}, u32[]{:S(2)}) async-start(bf16[4,2,7200]{2,1,0:T(2,128)(2,1)} %reshape.95), calls=%async_computation.1 | async-start | bytes 233472 | tf_op jit(solution)/shard_map/all_to_all | solution.py:45
  15.4 21.6 %all-to-all-start = ((bf16[4,2,7200]{2,1,0:T(2,128)(2,1)}), bf16[4,2,7200]{2,1,0:T(2,128)(2,1)S(1)}, u32[]{:S(2)}, u32[]{:S(2)}) async-start(bf16[4,2,7200]{2,1,0:T(2,128)(2,1)} %reshape.97), calls=%async_computation | async-start | bytes 233472 | tf_op jit(solution)/shard_map/all_to_all | solution.py:44
  38.2 0.6 copy-start.2
  55.1 0.8 copy-start.11
  55.8 0.8 copy-start.12
  56.6 1.0 copy-start.6
  56.6 1.0 copy-start.9
  57.6 0.7 copy-start.4
  60.4 3.5 %copy-start.3 = (bf16[32,15,120]{2,0,1:T(8,128)(2,1)S(1)}, bf16[32,15,120]{2,0,1:T(8,128)(2,1)}, u32[]{:S(2)}) copy-start(bf16[32,15,120]{2,0,1:T(8,128)(2,1)} %copy-done.2) | copy-start | bytes 345604
  60.4 20.2 %all-to-all-start.3 = ((bf16[4,2,7200]{2,1,0:T(2,128)(2,1)}), bf16[4,2,7200]{2,1,0:T(2,128)(2,1)S(1)}, u32[]{:S(2)}, u32[]{:S(2)}) async-start(bf16[4,2,7200]{2,1,0:T(2,128)(2,1)} %reshape.101), calls=%async_computation.3 | async-start | bytes 233472 | tf_op jit(solution)/shard_map/all_to_all | solution.py:65
  100.5 9.2 %all-to-all-start.4 = ((bf16[4,2,7200]{2,1,0:T(2,128)(2,1)}), bf16[4,2,7200]{2,1,0:T(2,128)(2,1)S(1)}, u32[]{:S(2)}, u32[]{:S(2)}) async-start(bf16[4,2,7200]{2,1,0:T(2,128)(2,1)} %reshape.105), calls=%async_computation.4 | async-start | bytes 233472 | tf_op jit(solution)/shard_map/all_to_all | solution.py:77
  104.7 1.2 copy-start.8
  109.7 8.3 %all-to-all-start.5 = ((bf16[4,2,7200]{2,1,0:T(2,128)(2,1)}), bf16[4,2,7200]{2,1,0:T(2,128)(2,1)S(1)}, u32[]{:S(2)}, u32[]{:S(2)}) async-start(bf16[4,2,7200]{2,1,0:T(2,128)(2,1)} %reshape.103), calls=%async_computation.5 | async-start | bytes 233472 | tf_op jit(solution)/shard_map/all_to_all | solution.py:80
  121.5 0.9 copy-start.5
  121.5 1.1 copy-start.7
  121.5 1.1 copy-start.10
where the time goes:
time: 125 us; the launch traced here: 124 us
  blocking collectives  59.2 us (47%)
  local copies, waits for them, and re-layouts  29.6 us (24%)
  starting transfers between devices  19.7 us (16%)
  waiting for transfers between devices  6.2 us (5%)
  matrix products  4.56 us (4%)
  other arithmetic  3.66 us (3%)
    all_gather x1, blocking collectives, on_device(): lax.all_gather(right_rows, 'dap', axis=1, tiled=True)  17 us
    all_gather x1, blocking collectives, on_device(): piece_left = lax.all_gather(left_rows, 'dap', axis=1, tiled=True)  16.8 us
    all_gather x1, blocking collectives, on_device(): piece_grad = lax.all_gather(grad_rows, 'dap', axis=1, tiled=True)  16.5 us
    unnamed x40, local copies, waits for them, and re-layouts  13.1 us
    all_to_all x1, blocking collectives, on_device(): lax.all_to_all(product, 'ch', split_axis=2, concat_axis=0, tiled=True)  8.94 us
    all_to_all x1, starting transfers between devices, on_device(): lax.all_to_all(right_cells, 'ch', split_axis=0, concat_axis=2, tiled=True)  5.19 us
    convert_element_type x3, local copies, waits for them, and re-layouts, on_device(): hidden_norm, hidden_scale = normalize(product_cells.astype(jnp.float32), 0)  4.68 us
    all_to_all x1, starting transfers between devices, on_device(): lax.all_to_all(new_left.astype(jnp.bfloat16), 'ch', split_axis=2, concat_...  4.21 us
  transfers between devices with their start and end apart: 5, of which 3 were waited for; matrix products, arithmetic and copies ran while one was open for 7% of the time, Pallas kernels for 0%

commit v1 on v0

--- a/solution.py
+++ b/solution.py
@@ -2,6 +2,7 @@
 import jax.numpy as jnp
 from jax import lax
 from jax.sharding import PartitionSpec as P
+from jax.lax import all_gather
 
 EPSILON = 1e-05
 
@@ -64,8 +65,11 @@
     grad_product = norm_back(grad_hidden, hidden_norm, hidden_scale, 0).astype(jnp.bfloat16)
     grad_rows = lax.all_to_all(grad_product, "ch", split_axis=0, concat_axis=2, tiled=True)
     piece_left = lax.all_gather(left_rows, "dap", axis=1, tiled=True)
-    piece_right = lax.all_gather(right_rows, "dap", axis=1, tiled=True)
-    piece_grad = lax.all_gather(grad_rows, "dap", axis=1, tiled=True)
+    piece_right, piece_grad = jnp.split(
+        all_gather(jnp.concatenate([right_rows, grad_rows], 0), "dap", axis=1, tiled=True),
+        [right_rows.shape[0]],
+        axis=0,
+    )
     cross_slab = lax.dynamic_slice_in_dim(piece_grad, row_start, row_count, 2)
     new_left = jnp.einsum(
         "cij,cjk->cik", grad_rows, piece_right, preferred_element_type=jnp.float32

time: 125 us -> 140 us (1.12)
  between operations: 1.06 us -> 14.5 us
  waiting for transfers between devices: 6.2 us -> 15.2 us
  blocking collectives: 59.2 us -> 54.2 us
  starting transfers between devices: 19.7 us -> 15.4 us
  local copies, waits for them, and re-layouts: 29.6 us -> 25.9 us
  other arithmetic: 3.66 us -> 6.96 us
  matrix products: 4.56 us -> 7.02 us
    all_gather x1 -> x0, blocking collectives: 16.5 us -> none  [on_device(): piece_grad = lax.all_gather(grad_rows, 'dap', axis=1, tiled=True)]
    all_gather x0 -> x1, waiting for transfers between devices: none -> 9.69 us  [on_device(): all_gather(jnp.concatenate([right_rows, grad_rows], 0), 'dap', axis=1, ti...]
    all_to_all x0 -> x1, blocking collectives: none -> 7.37 us  [on_device(): lax.all_to_all(grad_product, 'ch', split_axis=0, concat_axis=2, tiled=True)]
    all_gather x1, blocking collectives: 16.8 us -> 20.9 us  [on_device(): piece_left = lax.all_gather(left_rows, 'dap', axis=1, tiled=True)]
    all_to_all x1 -> x0, starting transfers between devices: 3.45 us -> none  [on_device(): lax.all_to_all(grad_product, 'ch', split_axis=0, concat_axis=2, tiled=True)]
    unnamed x40 -> x34, local copies, waits for them, and re-layouts: 13.1 us -> 9.88 us
    convert_element_type x3, local copies, waits for them, and re-layouts: 4.68 us -> 2.36 us  [on_device(): hidden_norm, hidden_scale = normalize(product_cells.astype(jnp.float32), 0)]
    split x0 -> x1, local copies, waits for them, and re-layouts: none -> 1.86 us  [on_device(): jnp.split(all_gather(jnp.concatenate([right_rows, grad_rows], 0), 'dap',...]
  transfers between devices with their start and end apart: 5 -> 5, of which waited for: 3 -> 4; matrix products, arithmetic and copies ran while one was open for 7% -> 7% of each run, Pallas kernels for 0% -> 0%
where the time goes in v1:
time: 140 us; the launch traced here: 139 us
  blocking collectives  54.2 us (39%)
  local copies, waits for them, and re-layouts  25.9 us (18%)
  starting transfers between devices  15.4 us (11%)
  waiting for transfers between devices  15.2 us (11%)
  between operations  14.5 us (10%)
  matrix products  7.02 us (5%)
  other arithmetic  6.96 us (5%)
    all_gather x1, blocking collectives, on_device(): piece_left = lax.all_gather(left_rows, 'dap', axis=1, tiled=True)  20.9 us
    all_gather x1, blocking collectives, on_device(): lax.all_gather(right_rows, 'dap', axis=1, tiled=True)  17 us
    unnamed x34, local copies, waits for them, and re-layouts  9.88 us
    all_gather x1, waiting for transfers between devices, on_device(): all_gather(jnp.concatenate([right_rows, grad_rows], 0), 'dap', axis=1, ti...  9.69 us
    all_to_all x1, blocking collectives, on_device(): lax.all_to_all(product, 'ch', split_axis=2, concat_axis=0, tiled=True)  8.89 us
    all_to_all x1, blocking collectives, on_device(): lax.all_to_all(grad_product, 'ch', split_axis=0, concat_axis=2, tiled=True)  7.37 us
    all_to_all x1, starting transfers between devices, on_device(): lax.all_to_all(right_cells, 'ch', split_axis=0, concat_axis=2, tiled=True)  5.19 us
    all_to_all x1, starting transfers between devices, on_device(): lax.all_to_all(new_right.astype(jnp.bfloat16), 'ch', split_axis=2, concat...  3.54 us
  transfers between devices with their start and end apart: 5, of which 4 were waited for; matrix products, arithmetic and copies ran while one was open for 7% of the time, Pallas kernels for 0%

profile of v1, /device:TPU:0, one launch (start us, length us, event | category | flops | bytes accessed | tf_op | source)
XLA Modules:
  0.0 139.2 jit_solution(12418385377730111434)
XLA Ops:
  8.3 1.2 fusion.24
  10.3 1.2 convolution_bitcast_fusion
  12.2 1.3 reshape.95
  13.5 5.2 %all-to-all-start.1 = ((bf16[4,2,7200]{2,1,0:T(2,128)(2,1)}), bf16[4,2,7200]{2,1,0:T(2,128)(2,1)S(1)}, u32[]{:S(2)}, u32[]{:S(2)}) async-start(bf16[4,2,7200]{2,1,0:T(2,128)(2,1)} %reshape.95), calls=%async_computation.1 | async-start | bytes 233472 | tf_op jit(solution)/shard_map/all_to_all | solution.py:46
  19.2 1.3 reshape.97
  20.5 3.2 %all-to-all-done.1 = bf16[4,2,7200]{2,1,0:T(2,128)(2,1)S(1)} async-done(((bf16[4,2,7200]{2,1,0:T(2,128)(2,1)}), bf16[4,2,7200]{2,1,0:T(2,128)(2,1)S(1)}, u32[]{:S(2)}, u32[]{:S(2)}) %all-to-all-start.1) | async-done | bytes 115232 | tf_op jit(solution)/shard_map/all_to_all | solution.py:46
  23.7 3.3 %all-to-all-start = ((bf16[4,2,7200]{2,1,0:T(2,128)(2,1)}), bf16[4,2,7200]{2,1,0:T(2,128)(2,1)S(1)}, u32[]{:S(2)}, u32[]{:S(2)}) async-start(bf16[4,2,7200]{2,1,0:T(2,128)(2,1)} %reshape.97), calls=%async_computation | async-start | bytes 233472 | tf_op jit(solution)/shard_map/all_to_all | solution.py:45
  28.3 17.0 %all_gather.9 = bf16[32,120,120]{2,0,1:T(8,128)(2,1)S(1)} all-gather(bf16[32,15,120]{2,0,1:T(8,128)(2,1)S(1)} %all_to_all.67), channel_id=1, replica_groups=mesh['dap'=8,'ch'=4] {'dap'}, dimensions={1}, use_global_device_ids=true | all-gather | bytes 1036800 | tf_op jit(solution)/shard_map/all_gather | solution.py:51
  48.1 8.9 %all_to_all.81 = bf16[4,2,7200]{2,1,0:T(2,128)(2,1)S(1)} all-to-all(bf16[4,2,7200]{2,1,0:T(2,128)(2,1)S(1)} %reshape.99), channel_id=1, replica_groups=mesh['dap'=8,'ch'=4] {'ch'}, dimensions={0} | all-to-all | bytes 230400 | tf_op jit(solution)/shard_map/all_to_all | solution.py:54
  58.5 1.5 %copy.81 = f32[4,32,15,30]{1,0,3,2:T(4,128)S(1)} copy(f32[4,32,15,30]{3,0,1,2:T(4,128)S(1)} %bitcast.66) | data formatting | bytes 460800 | tf_op jit(solution)/shard_map/convert_element_type | solution.py:55
  61.9 1.8 %multiply_convert_fusion.5 = (bf16[15,30,128]{2,1,0:T(8,128)(2,1)}, f32[15,30,128]{2,1,0:T(8,128)S(1)}) fusion(f32[15,30,128]{2,1,0:T(8,128)S(1)} %fusion.40, bf16[128,128]{1,0:T(8,128)(2,1)} %param.9, bf16[15,30,128]{2,1,0:T(8,128)(2,1)S(1)} %copy-done.1, f32[15,30]{1,0:T(8,128)S(1)} %add_rsqrt_fusion.1, f32[15,30]{1,0:T(8,128)S(1)} %broadcast_multiply_fusion.6), kind=kOutput, calls=%fused_computation.59 | convolution fusion | flops 15264000 | bytes 727568 | tf_op jit(solution)/shard_map/rkd,de->rke/dot_general | solution.py:42
  65.6 7.4 %all_to_all.82 = bf16[4,2,7200]{2,1,0:T(2,128)(2,1)S(1)} all-to-all(bf16[4,2,7200]{2,1,0:T(2,128)(2,1)S(1)} %reshape.101), channel_id=1, replica_groups=mesh['dap'=8,'ch'=4] {'ch'}, dimensions={0} | all-to-all | bytes 230400 | tf_op jit(solution)/shard_map/all_to_all | solution.py:66
  75.0 20.9 %all_gather.11 = bf16[32,120,120]{2,0,1:T(8,128)(2,1)} all-gather(bf16[32,15,120]{2,0,1:T(8,128)(2,1)S(1)} %all_to_all.63), channel_id=1, replica_groups=mesh['dap'=8,'ch'=4] {'dap'}, dimensions={1}, use_global_device_ids=true | all-gather | bytes 1036800 | tf_op jit(solution)/shard_map/all_gather | solution.py:67
  95.8 9.7 %all-gather.2.cloned.1.call-done = bf16[64,120,120]{2,0,1:T(8,128)(2,1)} async-done(((bf16[64,15,120]{2,0,1:T(8,128)(2,1)}), bf16[64,120,120]{2,0,1:T(8,128)(2,1)}) %all-gather.2.cloned.1.call-update) | async-done | bytes 1843216 | tf_op jit(solution)/shard_map/all_gather | solution.py:69
  105.5 1.9 %fusion.57 = (bf16[32,120,120]{2,0,1:T(8,128)(2,1)S(1)}, bf16[32,120,120]{2,0,1:T(8,128)(2,1)S(1)}) fusion(bf16[64,120,120]{2,0,1:T(8,128)(2,1)} %all-gather.2.cloned.1.call-done), kind=kLoop, calls=%fused_computation.91 | loop fusion | bytes 3686400 | tf_op jit(solution)/shard_map/split | solution.py:68
  108.4 1.1 reshape.105
  109.5 3.3 %all-to-all-start.4 = ((bf16[4,2,7200]{2,1,0:T(2,128)(2,1)}), bf16[4,2,7200]{2,1,0:T(2,128)(2,1)S(1)}, u32[]{:S(2)}, u32[]{:S(2)}) async-start(bf16[4,2,7200]{2,1,0:T(2,128)(2,1)} %reshape.105), calls=%async_computation.4 | async-start | bytes 233472 | tf_op jit(solution)/shard_map/all_to_all | solution.py:81
  115.2 1.1 reshape.103
  116.3 1.5 %all-to-all-done.4 = bf16[4,2,7200]{2,1,0:T(2,128)(2,1)S(1)} async-done(((bf16[4,2,7200]{2,1,0:T(2,128)(2,1)}), bf16[4,2,7200]{2,1,0:T(2,128)(2,1)S(1)}, u32[]{:S(2)}, u32[]{:S(2)}) %all-to-all-start.4) | async-done | bytes 115232 | tf_op jit(solution)/shard_map/all_to_all | solution.py:81
  117.8 3.5 %all-to-all-start.5 = ((bf16[4,2,7200]{2,1,0:T(2,128)(2,1)}), bf16[4,2,7200]{2,1,0:T(2,128)(2,1)S(1)}, u32[]{:S(2)}, u32[]{:S(2)}) async-start(bf16[4,2,7200]{2,1,0:T(2,128)(2,1)} %reshape.103), calls=%async_computation.5 | async-start | bytes 233472 | tf_op jit(solution)/shard_map/all_to_all | solution.py:84
  122.7 1.5 %copy.88 = f32[4,32,15,30]{1,0,3,2:T(4,128)S(1)} copy(f32[4,32,15,30]{3,0,1,2:T(4,128)S(1)} %bitcast.67) | data formatting | bytes 460800 | tf_op jit(solution)/shard_map/convert_element_type | solution.py:88
  124.1 1.1 reshape.86
  127.4 1.5 %copy.93 = f32[4,32,15,30]{1,0,3,2:T(4,128)S(1)} copy(f32[4,32,15,30]{3,0,1,2:T(4,128)S(1)} %bitcast.68) | data formatting | bytes 460800 | tf_op jit(solution)/shard_map/convert_element_type | solution.py:89
  129.3 1.3 multiply_convert_fusion.3
  (80 shorter events, 23.1 us)
Async XLA Ops:
  7.2 3.1 %copy-start = (bf16[128,512]{1,0:T(8,128)(2,1)S(1)}, bf16[128,512]{1,0:T(8,128)(2,1)}, u32[]{:S(2)}) copy-start(bf16[128,512]{1,0:T(8,128)(2,1)} %param.8) | copy-start | bytes 393220
  13.5 10.2 %all-to-all-start.1 = ((bf16[4,2,7200]{2,1,0:T(2,128)(2,1)}), bf16[4,2,7200]{2,1,0:T(2,128)(2,1)S(1)}, u32[]{:S(2)}, u32[]{:S(2)}) async-start(bf16[4,2,7200]{2,1,0:T(2,128)(2,1)} %reshape.95), calls=%async_computation.1 | async-start | bytes 233472 | tf_op jit(solution)/shard_map/all_to_all | solution.py:46
  23.7 21.6 %all-to-all-start = ((bf16[4,2,7200]{2,1,0:T(2,128)(2,1)}), bf16[4,2,7200]{2,1,0:T(2,128)(2,1)S(1)}, u32[]{:S(2)}, u32[]{:S(2)}) async-start(bf16[4,2,7200]{2,1,0:T(2,128)(2,1)} %reshape.97), calls=%async_computation | async-start | bytes 233472 | tf_op jit(solution)/shard_map/all_to_all | solution.py:45
  27.0 78.5 %all-gather.2.cloned.1.call-start = ((), (), s32[]{:S(2)}) async-start(), calls=%async_computation.6 | async-start | bytes 2211840 | tf_op jit(solution)/shard_map/all_gather | solution.py:69
  28.3 18.9 %copy-start.2 = (bf16[32,15,120]{2,0,1:T(8,128)(2,1)}, bf16[32,15,120]{2,0,1:T(8,128)(2,1)S(1)}, u32[]{:S(2)}) copy-start(bf16[32,15,120]{2,0,1:T(8,128)(2,1)S(1)} %all_to_all.67) | copy-start | bytes 345604
  58.5 3.4 %copy-start.1 = (bf16[15,30,128]{2,1,0:T(8,128)(2,1)S(1)}, bf16[15,30,128]{2,1,0:T(8,128)(2,1)}, u32[]{:S(2)}) copy-start(bf16[15,30,128]{2,1,0:T(8,128)(2,1)} %param.6) | copy-start | bytes 345604
  60.4 3.2 %copy-start.7 = (bf16[15,30,128]{2,1,0:T(8,128)(2,1)S(1)}, bf16[15,30,128]{2,1,0:T(8,128)(2,1)}, u32[]{:S(2)}) copy-start(bf16[15,30,128]{2,1,0:T(8,128)(2,1)} %param.11) | copy-start | bytes 345604
  60.4 3.2 %copy-start.9 = (bf16[128,128]{1,0:T(8,128)(2,1)S(1)}, bf16[128,128]{1,0:T(8,128)(2,1)}, u32[]{:S(2)}) copy-start(bf16[128,128]{1,0:T(8,128)(2,1)} %param.10) | copy-start | bytes 98308
  61.9 2.2 %copy-start.4 = (f32[15,30,128]{2,1,0:T(8,128)}, f32[15,30,128]{2,1,0:T(8,128)S(1)}, u32[]{:S(2)}) copy-start(f32[15,30,128]{2,1,0:T(8,128)S(1)} %fusion.40) | copy-start | bytes 691204
  64.4 9.7 %copy-start.3 = (bf16[32,15,120]{2,0,1:T(8,128)(2,1)S(1)}, bf16[32,15,120]{2,0,1:T(8,128)(2,1)}, u32[]{:S(2)}) copy-start(bf16[32,15,120]{2,0,1:T(8,128)(2,1)} %copy-done.2) | copy-start | bytes 345604
  109.5 8.3 %all-to-all-start.4 = ((bf16[4,2,7200]{2,1,0:T(2,128)(2,1)}), bf16[4,2,7200]{2,1,0:T(2,128)(2,1)S(1)}, u32[]{:S(2)}, u32[]{:S(2)}) async-start(bf16[4,2,7200]{2,1,0:T(2,128)(2,1)} %reshape.105), calls=%async_computation.4 | async-start | bytes 233472 | tf_op jit(solution)/shard_map/all_to_all | solution.py:81
  112.8 1.2 copy-start.6
  117.8 8.3 %all-to-all-start.5 = ((bf16[4,2,7200]{2,1,0:T(2,128)(2,1)}), bf16[4,2,7200]{2,1,0:T(2,128)(2,1)S(1)}, u32[]{:S(2)}, u32[]{:S(2)}) async-start(bf16[4,2,7200]{2,1,0:T(2,128)(2,1)} %reshape.103), calls=%async_computation.5 | async-start | bytes 233472 | tf_op jit(solution)/shard_map/all_to_all | solution.py:84
  129.3 1.6 %copy-start.5 = (f32[15,30,128]{2,1,0:T(8,128)S(1)}, f32[15,30,128]{2,1,0:T(8,128)}, u32[]{:S(2)}) copy-start(f32[15,30,128]{2,1,0:T(8,128)} %copy-done.4) | copy-start | bytes 691204
  129.3 1.6 %copy-start.8 = (bf16[15,30,128]{2,1,0:T(8,128)(2,1)S(1)}, bf16[15,30,128]{2,1,0:T(8,128)(2,1)}, u32[]{:S(2)}) copy-start(bf16[15,30,128]{2,1,0:T(8,128)(2,1)} %param.11) | copy-start | bytes 345604
  129.3 1.6 %copy-start.10 = (bf16[128,128]{1,0:T(8,128)(2,1)S(1)}, bf16[128,128]{1,0:T(8,128)(2,1)}, u32[]{:S(2)}) copy-start(bf16[128,128]{1,0:T(8,128)(2,1)} %param.9) | copy-start | bytes 98308
Sparse Core Ops, SparseCore 0:
  75.1 30.4 all-gather.1
